TPU v7x, 256 devices: a whole 4x4x8 slice. The times are simulated.
256 devices in a mesh: expert: 32 (over z, x), tensor: 8 (over y, core).
Axes of the slice: x: 4, y: 4, z: 8, core: 2. Of those that a mesh axis runs over, the one named last changes fastest.
Arguments:
- query_latent: bfloat16 [1024, 64, 576], P(('expert', 'tensor')), may hold values from -9 to 9
- kv_cache: bfloat16 [1024, 768, 576], P(('expert', 'tensor')), may hold values from -4 to 4
- cache_len: int32 [1024], P(('expert', 'tensor')), may hold values from 192 to 768, as said below
- value_up: bfloat16 [64, 512, 128], P('tensor'), may hold values from -0.25 to 0.25
- hidden_in: bfloat16 [1024, 7168], P('expert', 'tensor'), may hold values from -6 to 6
- norm_gain: bfloat16 [7168], P('tensor'), may hold values from 0.099609375 to 1.8984375
- expert_ids: int32 [1024, 8], P('expert'), may hold values from 0 to 29, all different within a row; in each aligned block of 32 rows (0 to 31, 32 to 63, ...) at most 18 rows name the same one
- route_weight: int32 [1024, 8], P('expert'), may hold values from 1 to 4095
- placement_plan: int32 [32], replicated, may hold values from 0 to 29, as said below
- updated_list: int32 [30], replicated, may hold values from 0 to 29, each once
- learner_gate: bfloat16 [30, 7168, 1024], P(None, 'expert', 'tensor'), may hold values from -0.0625 to 0.0625
- learner_up: bfloat16 [30, 7168, 1024], P(None, 'expert', 'tensor'), may hold values from -0.0625 to 0.0625
- learner_down: bfloat16 [30, 7168, 1024], P(None, 'expert', 'tensor'), may hold values from -0.1875 to 0.1875
Outputs:
- attn_values: bfloat16 [1024, 8192], P('expert', 'tensor')
- moe_out: bfloat16 [1024, 7168], P('expert', 'tensor')
- slot_gate: bfloat16 [32, 7168, 1024], P('expert', None, 'tensor')
Inputs may be any that keep to these rules, and one draw needn't show every extreme that they name: `cache_len`: some row has all 768 positions valid. `placement_plan`: every expert is held by one or two slots; 2 experts by two. `expert_ids`: each row names 8 different experts; among the 32 rows of one device no expert is named more than 18 times. `updated_list`: each expert once.
All inputs are finite; a program needn't handle non-finite values.
Results may differ from a plain program's by a relative error of at most 0.015.
Values may be sent and summed in bfloat16 or wider, within the bound.
No kernel may reach another device: no remote copies, remote signals or barrier semaphores. Data moves between devices by JAX's collectives and lax.ppermute only.
A program may use at most 128 MiB of HBM per device.

v0:
```python
import jax
import jax.numpy as jnp
from jax import lax
from jax.sharding import PartitionSpec as P

KVL = 512
SCORE_SCALE = 192.0 ** (-0.5)
ROUTE_SCALE = 2.5
NORM_EPSILON = 1e-06


def attend(query_latent, kv_cache, cache_len):
    scores = (
        jnp.einsum("rhc,rpc->rhp", query_latent, kv_cache, preferred_element_type=jnp.float32)
        * SCORE_SCALE
    )
    allowed = (jnp.arange(kv_cache.shape[1], dtype=jnp.int32)[None, :] < cache_len[:, None])[
        :, None, :
    ]
    scores = jnp.where(allowed, scores, -1e30)
    highest = jnp.max(scores, axis=2, keepdims=True)
    lifted = jnp.where(allowed, jnp.exp(scores - highest), 0.0)
    totals = jnp.sum(lifted, axis=2, keepdims=True)
    mixed = jnp.einsum(
        "rhp,rpc->rhc",
        lifted.astype(jnp.bfloat16),
        kv_cache[:, :, :KVL],
        preferred_element_type=jnp.float32,
    )
    return (mixed / totals).astype(jnp.bfloat16)


def route_targets(expert_ids, placement_plan, expert_total, capacity):
    row_count, choose_count = expert_ids.shape
    entries = row_count * choose_count
    slot_total = placement_plan.shape[0]
    flat_ids = expert_ids.reshape(entries)
    expert_range = jnp.arange(expert_total, dtype=jnp.int32)
    holders = (placement_plan[None, :] == expert_range[:, None]).astype(jnp.int32)
    holder_rank = jnp.cumsum(holders, axis=1) - 1
    picked = (flat_ids[:, None] == expert_range[None, :]).astype(jnp.int32)
    entry_hold = jnp.dot(picked, holders)
    entry_rank = jnp.dot(picked, holder_rank)
    matched = entry_hold * (entry_rank == 0).astype(jnp.int32)
    slot_index = jnp.sum(matched * jnp.arange(slot_total, dtype=jnp.int32)[None, :], axis=1)
    position = jnp.sum(matched * (jnp.cumsum(matched, axis=0) - 1), axis=1)
    return slot_index * capacity + position


def per_device(
    query_latent,
    kv_cache,
    cache_len,
    value_up,
    hidden_in,
    norm_gain,
    expert_ids,
    route_weight,
    placement_plan,
    updated_list,
    learner_gate,
    learner_up,
    learner_down,
):
    expert_total = updated_list.shape[0]
    entry_range = jnp.arange(expert_total, dtype=jnp.int32)
    learner_entry = jnp.sum(
        entry_range[None, :] * (updated_list[None, :] == placement_plan[:, None]).astype(jnp.int32),
        axis=1,
    )
    held_gate, held_up = (
        lax.all_to_all(
            jnp.take(learner_gate, learner_entry, axis=0),
            "expert",
            split_axis=0,
            concat_axis=1,
            tiled=True,
        ),
        lax.all_to_all(
            jnp.take(learner_up, learner_entry, axis=0),
            "expert",
            split_axis=0,
            concat_axis=1,
            tiled=True,
        ),
    )
    chosen_down = jnp.take(learner_down, learner_entry, axis=0)
    held_down = lax.all_to_all(chosen_down, "expert", split_axis=0, concat_axis=1, tiled=True)
    latent = attend(query_latent, kv_cache, cache_len)
    head_rows = lax.all_to_all(latent, "tensor", split_axis=1, concat_axis=0, tiled=True)
    projected = jnp.einsum("rhc,hcv->rhv", head_rows, value_up, preferred_element_type=jnp.float32)
    attn_values = projected.astype(jnp.bfloat16).reshape(
        head_rows.shape[0], projected.shape[1] * projected.shape[2]
    )
    row_count, choose_count = expert_ids.shape
    slot_total = placement_plan.shape[0]
    capacity = min(row_count, 2 * ((row_count * choose_count + expert_total - 1) // expert_total))
    targets = route_targets(expert_ids, placement_plan, expert_total, capacity)
    entry_row = jnp.arange(row_count * choose_count, dtype=jnp.int32) // choose_count
    whole_rows, whole_gain = (
        lax.all_gather(hidden_in, "tensor", axis=1, tiled=True),
        lax.all_gather(norm_gain.reshape(1, norm_gain.shape[0]), "tensor", axis=1, tiled=True),
    )
    widened = whole_rows.astype(jnp.float32)
    normed = (
        widened
        * lax.rsqrt(jnp.mean(widened * widened, axis=1, keepdims=True) + NORM_EPSILON)
        * whole_gain.astype(jnp.float32)
    ).astype(jnp.bfloat16)
    outbound = (
        jnp.zeros((slot_total * capacity, normed.shape[1]), jnp.bfloat16)
        .at[targets]
        .set(normed[entry_row])
    )
    arrived = lax.all_to_all(outbound, "expert", split_axis=0, concat_axis=0, tiled=True)
    gate_proj = jnp.dot(arrived, held_gate[0], preferred_element_type=jnp.float32)
    up_proj = jnp.dot(arrived, held_up[0], preferred_element_type=jnp.float32)
    activated = (jax.nn.silu(gate_proj) * up_proj).astype(jnp.bfloat16)
    partial_out = lax.dot_general(
        activated, held_down[0], (((1,), (1,)), ((), ())), preferred_element_type=jnp.float32
    )
    shared = lax.psum_scatter(
        partial_out.astype(jnp.bfloat16), "tensor", scatter_dimension=1, tiled=True
    )
    returned = lax.all_to_all(shared, "expert", split_axis=0, concat_axis=0, tiled=True)
    entry_out = (
        returned[targets].astype(jnp.float32).reshape(row_count, choose_count, returned.shape[1])
    )
    weights_float = route_weight.astype(jnp.float32)
    gates = ROUTE_SCALE * weights_float / jnp.sum(weights_float, axis=1, keepdims=True)
    moe_out = jnp.sum(gates[:, :, None] * entry_out, axis=1).astype(jnp.bfloat16)
    return (attn_values, moe_out, held_gate)


def solution(mesh):
    in_specs = (
        P(("expert", "tensor"), None, None),
        P(("expert", "tensor"), None, None),
        P(("expert", "tensor")),
        P("tensor", None, None),
        P("expert", "tensor"),
        P("tensor"),
        P("expert", None),
        P("expert", None),
        P(),
        P(),
        P(None, "expert", "tensor"),
        P(None, "expert", "tensor"),
        P(None, "expert", "tensor"),
    )
    out_specs = (P("expert", "tensor"), P("expert", "tensor"), P("expert", None, "tensor"))
    return jax.shard_map(
        per_device, mesh=mesh, in_specs=in_specs, out_specs=out_specs, check_vma=False
    )
```

profile of v0, /device:TPU:2, one launch (start us, length us, event | category | flops | bytes accessed | tf_op | source)
XLA Modules:
  0.0 589.7 jit_solution(17599667615994118623)
XLA Ops:
  7.2 0.0 copy-start
  7.2 1.0 select_reduce_fusion
  8.2 0.5 compare_and_fusion
  8.7 0.6 pad_clamp_fusion.1
  9.3 1.0 gather_fusion.1
  10.3 0.0 copy-start.4
  10.3 3.7 gather_fusion.2
  14.1 0.0 copy-done.4
  14.1 2.1 gather_fusion.3
  16.2 4.8 broadcast_select_fusion.2
  21.0 11.7 %all-to-all-start.2 = ((bf16[32,224,128]{2,1,0:T(8,128)(2,1)}), bf16[32,224,128]{2,1,0:T(8,128)(2,1)S(1)}, u32[]{:S(2)}, u32[]{:S(2)}) async-start(bf16[32,224,128]{2,1,0:T(8,128)(2,1)} %get-tuple-element.6), calls=%async_computation.2 | async-start | bytes 3670016 | tf_op jit(solution)/shard_map/all_to_all | solution.py:72
  32.7 0.1 copy.41
  32.8 0.1 eq.49
  32.9 0.0 copy-done.10
  32.9 0.2 reduce_window_sum.24
  33.1 43.4 %all-to-all-done.2 = bf16[32,224,128]{2,1,0:T(8,128)(2,1)S(1)} async-done(((bf16[32,224,128]{2,1,0:T(8,128)(2,1)}), bf16[32,224,128]{2,1,0:T(8,128)(2,1)S(1)}, u32[]{:S(2)}, u32[]{:S(2)}) %all-to-all-start.2) | async-done | bytes 1835040 | tf_op jit(solution)/shard_map/all_to_all | solution.py:72
  76.5 1.2 copy-done.2
  77.8 6.7 %all-to-all-start.3 = ((bf16[32,224,128]{2,1,0:T(8,128)(2,1)}), bf16[32,224,128]{2,1,0:T(8,128)(2,1)S(1)}, u32[]{:S(2)}, u32[]{:S(2)}) async-start(bf16[32,224,128]{2,1,0:T(8,128)(2,1)} %get-tuple-element.7), calls=%async_computation.3 | async-start | bytes 3670016 | tf_op jit(solution)/shard_map/all_to_all | solution.py:79
  84.5 0.3 convolution_compare_fusion
  84.7 0.2 convolution_select_fusion
  85.0 0.6 reduce-window.6
  85.6 0.2 slice_reduce_fusion
  85.8 13.4 %all-gather.1 = bf16[8,1,896]{2,1,0:T(2,128)(2,1)S(1)} all-gather(bf16[1,1,896]{2,1,0:T(2,128)(2,1)S(1)} %reshape.212), channel_id=2, replica_groups=mesh['expert'=32,'tensor'=8] {'tensor'}, dimensions={0}, use_global_device_ids=true | all-gather | bytes 16128 | tf_op jit(solution)/shard_map/all_gather | solution.py:102
  99.3 0.1 multiply_reduce_fusion
  99.4 13.6 %all_gather.6 = bf16[32,7168]{1,0:T(8,128)(2,1)S(1)} all-gather(bf16[32,896]{1,0:T(8,128)(2,1)S(1)} %copy-done.6), channel_id=1, replica_groups=mesh['expert'=32,'tensor'=8] {'tensor'}, dimensions={1}, use_global_device_ids=true | all-gather | bytes 516096 | tf_op jit(solution)/shard_map/all_gather | solution.py:101
  112.9 0.2 fusion.18
  113.2 0.2 fusion.20
  113.4 20.7 %scatter_custom_fusion = bf16[576,7168]{1,0:T(8,128)(2,1)} fusion(s32[256]{0:T(256)S(1)} %bitcast.65, bf16[]{:T(256)} %constant.57.clone.1, bf16[32,7168]{1,0:T(8,128)(2,1)S(1)} %fusion.20, s32[1024]{0:T(1024)S(1)} %pad_clamp_fusion.2), kind=kCustom, calls=%fused_computation.8 | custom fusion | bytes 8257538 | tf_op jit(solution)/shard_map/scatter | solution.py:113
  134.1 10.4 %all_to_all.56 = bf16[32,18,7168]{2,1,0:T(8,128)(2,1)} reshape(bf16[576,7168]{1,0:T(8,128)(2,1)} %scatter_custom_fusion) | data formatting | bytes 16515072 | tf_op jit(solution)/shard_map/all_to_all | solution.py:115
  144.5 0.0 all-to-all-done.3
  144.5 251.9 %all_to_all.72 = bf16[32,18,7168]{2,1,0:T(8,128)(2,1)} all-to-all(bf16[32,18,7168]{2,1,0:T(8,128)(2,1)} %all_to_all.56), channel_id=1, replica_groups=mesh['expert'=32,'tensor'=8] {'expert'}, dimensions={0} | all-to-all | bytes 16515072 | tf_op jit(solution)/shard_map/all_to_all | solution.py:115
  396.4 5.6 all-to-all-start.4
  402.1 0.3 reduce-scatter.4.cloned.1.call-start
  402.3 10.5 %all_to_all.58 = bf16[576,7168]{1,0:T(8,128)(2,1)} reshape(bf16[32,18,7168]{2,1,0:T(8,128)(2,1)} %all_to_all.72) | data formatting | bytes 16515072 | tf_op jit(solution)/shard_map/all_to_all | solution.py:115
  412.8 6.1 %fusion.40 = f32[576,128]{1,0:T(8,128)S(1)} fusion(bf16[576,7168]{1,0:T(8,128)(2,1)} %all_to_all.58, bf16[7168,128]{1,0:T(8,128)(2,1)} %bitcast.58), kind=kOutput, calls=%fused_computation.80 | convolution fusion | flops 1056964608 | bytes 10387456 | tf_op jit(solution)/shard_map/dot_general | solution.py:116
  419.0 27.4 %all-to-all-done.4 = bf16[32,224,128]{2,1,0:T(8,128)(2,1)} async-done(((bf16[32,224,128]{2,1,0:T(8,128)(2,1)}), bf16[32,224,128]{2,1,0:T(8,128)(2,1)}, u32[]{:S(2)}, u32[]{:S(2)}) %all-to-all-start.4) | async-done | bytes 1835040 | tf_op jit(solution)/shard_map/all_to_all | solution.py:88
  446.3 13.6 %convolution_convert_fusion = bf16[576,7168]{1,0:T(8,128)(2,1)} fusion(bf16[7168,128]{1,0:T(8,128)(2,1)} %bitcast.11, bf16[576,7168]{1,0:T(8,128)(2,1)} %all_to_all.58, bf16[7168,128]{1,0:T(8,128)(2,1)S(1)} %bitcast.57, f32[576,128]{1,0:T(8,128)S(1)} %fusion.40), kind=kOutput, calls=%fused_computation.7 | convolution fusion | flops 2118500352 | bytes 20480000 | tf_op jit(solution)/shard_map/dot_general | solution.py:119
  459.9 12.4 %copy.44 = bf16[576,7168]{0,1:T(8,128)(2,1)} copy(bf16[576,7168]{1,0:T(8,128)(2,1)} %convolution_convert_fusion) | data formatting | bytes 16515072
  472.3 0.0 reduce-scatter.4.cloned.1.call-update
  472.4 0.6 copy-done.11
  473.0 0.1 iota_compare_fusion.5
  473.1 0.3 copy-done.12
  473.3 3.0 fusion.39
  476.3 3.0 fusion.13
  479.3 0.9 copy.37
  480.2 3.6 all-to-all-start
  483.8 46.4 %reduce-scatter.4.cloned.1.call-done = bf16[896,576]{1,0:T(8,128)(2,1)} async-done(((bf16[7168,576]{1,0:T(8,128)(2,1)}), bf16[896,576]{1,0:T(8,128)(2,1)}) %reduce-scatter.4.cloned.1.call-update) | async-done | bytes 1032208
  530.2 1.7 copy.45
  531.9 1.3 all_to_all.62
  533.2 0.0 all-to-all-done
  533.2 10.2 %all-to-all-start.5 = ((bf16[32,18,896]{2,1,0:T(8,128)(2,1)}), bf16[32,18,896]{2,1,0:T(8,128)(2,1)S(1)}, u32[]{:S(2)}, u32[]{:S(2)}) async-start(bf16[32,18,896]{2,1,0:T(8,128)(2,1)} %all_to_all.62), calls=%async_computation.5 | async-start | bytes 2752512 | tf_op jit(solution)/shard_map/all_to_all | solution.py:125
  543.4 0.0 copy-done.7
  543.5 0.1 copy.40
  543.5 0.1 copy.54
  543.6 0.1 all_to_all.55
  543.7 0.3 fusion.17
  544.0 0.7 copy.55
  544.6 33.3 %all-to-all-done.5 = bf16[32,18,896]{2,1,0:T(8,128)(2,1)S(1)} async-done(((bf16[32,18,896]{2,1,0:T(8,128)(2,1)}), bf16[32,18,896]{2,1,0:T(8,128)(2,1)S(1)}, u32[]{:S(2)}, u32[]{:S(2)}) %all-to-all-start.5) | async-done | bytes 1032224 | tf_op jit(solution)/shard_map/all_to_all | solution.py:125
  578.0 0.3 all_to_all.64
  578.3 0.0 copy-start.3
  578.3 1.2 gather_fusion
  579.5 1.0 fusion.21
  580.5 1.2 copy.59
  581.7 0.9 copy-done.1
  (31 shorter events, 0.2 us)
Async XLA Ops:
  7.2 2.1 copy-start
  10.3 3.7 copy-start.4
  21.0 11.8 %copy-start.8 = (s32[32,8]{0,1:T(8,128)S(1)}, s32[32,8]{0,1:T(8,128)}, u32[]{:S(2)}) copy-start(s32[32,8]{0,1:T(8,128)} %param.21) | copy-start | bytes 3076
  21.0 11.9 %copy-start.10 = (s32[32]{0:T(128)S(1)}, s32[32]{0:T(128)}, u32[]{:S(2)}) copy-start(s32[32]{0:T(128)} %param.23) | copy-start | bytes 388
  21.0 55.5 %all-to-all-start.2 = ((bf16[32,224,128]{2,1,0:T(8,128)(2,1)}), bf16[32,224,128]{2,1,0:T(8,128)(2,1)S(1)}, u32[]{:S(2)}, u32[]{:S(2)}) async-start(bf16[32,224,128]{2,1,0:T(8,128)(2,1)} %get-tuple-element.6), calls=%async_computation.2 | async-start | bytes 3670016 | tf_op jit(solution)/shard_map/all_to_all | solution.py:72
  76.5 1.2 copy-start.2
  76.5 9.3 %copy-start.9 = (bf16[896]{0:T(1024)(128)(2,1)S(1)}, bf16[896]{0:T(1024)(128)(2,1)}, u32[]{:S(2)}) copy-start(bf16[896]{0:T(1024)(128)(2,1)} %param.20) | copy-start | bytes 5380
  76.5 22.9 %copy-start.6 = (bf16[32,896]{1,0:T(8,128)(2,1)S(1)}, bf16[32,896]{1,0:T(8,128)(2,1)}, u32[]{:S(2)}) copy-start(bf16[32,896]{1,0:T(8,128)(2,1)} %param.19) | copy-start | bytes 172036
  77.8 66.7 %all-to-all-start.3 = ((bf16[32,224,128]{2,1,0:T(8,128)(2,1)}), bf16[32,224,128]{2,1,0:T(8,128)(2,1)S(1)}, u32[]{:S(2)}, u32[]{:S(2)}) async-start(bf16[32,224,128]{2,1,0:T(8,128)(2,1)} %get-tuple-element.7), calls=%async_computation.3 | async-start | bytes 3670016 | tf_op jit(solution)/shard_map/all_to_all | solution.py:79
  396.4 49.9 %all-to-all-start.4 = ((bf16[32,224,128]{2,1,0:T(8,128)(2,1)}), bf16[32,224,128]{2,1,0:T(8,128)(2,1)}, u32[]{:S(2)}, u32[]{:S(2)}) async-start(bf16[32,224,128]{2,1,0:T(8,128)(2,1)} %get-tuple-element.8), calls=%async_computation.4 | async-start | bytes 3670016 | tf_op jit(solution)/shard_map/all_to_all | solution.py:88
  402.1 128.1 %reduce-scatter.4.cloned.1.call-start = ((), (), s32[]{:S(2)}) async-start(), calls=%async_computation.7 | async-start | bytes 10321920
  472.3 0.7 copy-start.11
  472.3 1.0 copy-start.12
  480.2 53.0 %all-to-all-start = ((bf16[4,64,512]{2,0,1:T(4,128)(2,1)}), bf16[4,64,512]{2,0,1:T(4,128)(2,1)S(1)}, u32[]{:S(2)}, u32[]{:S(2)}) async-start(bf16[4,64,512]{2,0,1:T(4,128)(2,1)} %copy.37), calls=%async_computation | async-start | bytes 524288 | tf_op jit(solution)/shard_map/all_to_all | solution.py:90
  533.2 10.3 %copy-start.7 = (s32[32,8]{0,1:T(8,128)S(1)}, s32[32,8]{0,1:T(8,128)}, u32[]{:S(2)}) copy-start(s32[32,8]{0,1:T(8,128)} %param.22) | copy-start | bytes 3076
  533.2 10.6 %copy-start.5 = (bf16[8,512,128]{2,1,0:T(8,128)(2,1)S(1)}, bf16[8,512,128]{2,1,0:T(8,128)(2,1)}, u32[]{:S(2)}) copy-start(bf16[8,512,128]{2,1,0:T(8,128)(2,1)} %param.18) | copy-start | bytes 3145732
  533.2 44.8 %all-to-all-start.5 = ((bf16[32,18,896]{2,1,0:T(8,128)(2,1)}), bf16[32,18,896]{2,1,0:T(8,128)(2,1)S(1)}, u32[]{:S(2)}, u32[]{:S(2)}) async-start(bf16[32,18,896]{2,1,0:T(8,128)(2,1)} %all_to_all.62), calls=%async_computation.5 | async-start | bytes 2752512 | tf_op jit(solution)/shard_map/all_to_all | solution.py:125
  578.3 2.2 copy-start.3
  580.5 2.1 copy-start.1
Sparse Core Ops, SparseCore 0:
  472.5 57.6 reduce-scatter.3
where the time goes:
time: 595 us; the launch traced here: 590 us
  blocking collectives  279 us (47%)
  waiting for transfers between devices  150 us (25%)
  local copies, waits for them, and re-layouts  71.8 us (12%)
  starting transfers between devices  38.2 us (6%)
  matrix products  26.5 us (4%)
  between operations  14.5 us (2%)
  other arithmetic  9.34 us (2%)
    all_to_all x1, blocking collectives, per_device(): lax.all_to_all(outbound, 'expert', split_axis=0, concat_axis=0, tiled=True)  252 us
    unnamed x2, waiting for transfers between devices  46.4 us
    all_to_all x1, waiting for transfers between devices, per_device(): lax.all_to_all(jnp.take(learner_gate, learner_entry, axis=0), 'expert', s...  43.4 us
    all_to_all x1, waiting for transfers between devices, per_device(): lax.all_to_all(shared, 'expert', split_axis=0, concat_axis=0, tiled=True)  33.3 us
    all_to_all x1, waiting for transfers between devices, per_device(): lax.all_to_all(chosen_down, 'expert', split_axis=0, concat_axis=1, tiled=...  27.4 us
    all_to_all x2, local copies, waits for them, and re-layouts, per_device(): lax.all_to_all(outbound, 'expert', split_axis=0, concat_axis=0, tiled=True)  20.9 us
    scatter x1, local copies, waits for them, and re-layouts, per_device(): outbound = jnp.zeros((slot_total * capacity, normed.shape[1]), jnp.bfloat...  20.7 us
    unnamed x31, local copies, waits for them, and re-layouts  18.5 us
  transfers between devices with their start and end apart: 6, of which 4 were waited for; matrix products, arithmetic and copies ran while one was open for 7% of the time, Pallas kernels for 0%

commit v1 on v0

--- a/solution.py
+++ b/solution.py
@@ -85,7 +85,12 @@
         ),
     )
     chosen_down = jnp.take(learner_down, learner_entry, axis=0)
-    held_down = lax.all_to_all(chosen_down, "expert", split_axis=0, concat_axis=1, tiled=True)
+    held_down = jnp.concatenate(
+        lax.all_to_all(
+            jnp.stack(jnp.split(chosen_down, lax.axis_size("expert"), axis=0)), "expert", 0, 0
+        ),
+        axis=1,
+    )
     latent = attend(query_latent, kv_cache, cache_len)
     head_rows = lax.all_to_all(latent, "tensor", split_axis=1, concat_axis=0, tiled=True)
     projected = jnp.einsum("rhc,hcv->rhv", head_rows, value_up, preferred_element_type=jnp.float32)

time: 595 us -> 614 us (1.032)
  local copies, waits for them, and re-layouts: 71.8 us -> 91.9 us
    all_to_all x1, waiting for transfers between devices: 43.4 us -> 0.01 us  [per_device(): lax.all_to_all(jnp.take(learner_gate, learner_entry, axis=0), 'expert', s...]
    all_to_all x1, waiting for transfers between devices: 0.01 us -> 27.3 us  [per_device(): lax.all_to_all(jnp.take(learner_up, learner_entry, axis=0), 'expert', spl...]
    unnamed x31 -> x64, local copies, waits for them, and re-layouts: 18.5 us -> 37.8 us
    all_to_all x1, waiting for transfers between devices: 27.4 us -> 43.4 us  [per_device(): lax.all_to_all(jnp.stack(jnp.split(chosen_down, lax.axis_size('expert'),...]
  transfers between devices with their start and end apart: 6 -> 6, of which waited for: 4 -> 4; matrix products, arithmetic and copies ran while one was open for 7% -> 6% of each run, Pallas kernels for 0% -> 0%
where the time goes in v1:
time: 614 us; the launch traced here: 609 us
  blocking collectives  279 us (45%)
  waiting for transfers between devices  150 us (24%)
  local copies, waits for them, and re-layouts  91.9 us (15%)
  starting transfers between devices  38.1 us (6%)
  matrix products  26.5 us (4%)
  between operations  14.5 us (2%)
  other arithmetic  9.08 us (1%)
    all_to_all x1, blocking collectives, per_device(): lax.all_to_all(outbound, 'expert', split_axis=0, concat_axis=0, tiled=True)  252 us
    unnamed x2, waiting for transfers between devices  46.4 us
    all_to_all x1, waiting for transfers between devices, per_device(): lax.all_to_all(jnp.stack(jnp.split(chosen_down, lax.axis_size('expert'),...  43.4 us
    unnamed x64, local copies, waits for them, and re-layouts  37.8 us
    all_to_all x1, waiting for transfers between devices, per_device(): lax.all_to_all(shared, 'expert', split_axis=0, concat_axis=0, tiled=True)  33.3 us
    all_to_all x1, waiting for transfers between devices, per_device(): lax.all_to_all(jnp.take(learner_up, learner_entry, axis=0), 'expert', spl...  27.3 us
    all_to_all x2, local copies, waits for them, and re-layouts, per_device(): lax.all_to_all(outbound, 'expert', split_axis=0, concat_axis=0, tiled=True)  20.9 us
    scatter x1, local copies, waits for them, and re-layouts, per_device(): outbound = jnp.zeros((slot_total * capacity, normed.shape[1]), jnp.bfloat...  20.7 us
  transfers between devices with their start and end apart: 6, of which 4 were waited for; matrix products, arithmetic and copies ran while one was open for 6% of the time, Pallas kernels for 0%

profile of v1, /device:TPU:2, one launch (start us, length us, event | category | flops | bytes accessed | tf_op | source)
XLA Modules:
  0.0 609.4 jit_solution(7263334805345788320)
XLA Ops:
  7.2 1.0 select_reduce_fusion
  9.3 1.0 gather_fusion.1
  10.3 3.7 gather_fusion.2
  14.1 2.2 gather_fusion.3
  16.3 4.5 broadcast_select_fusion.2
  20.8 0.6 constant_dynamic-update-slice_fusion.31
  22.0 0.6 constant_dynamic-update-slice_fusion.29
  22.7 0.6 constant_dynamic-update-slice_fusion.28
  23.3 0.6 constant_dynamic-update-slice_fusion.27
  23.9 0.6 constant_dynamic-update-slice_fusion.26
  24.5 0.6 constant_dynamic-update-slice_fusion.25
  25.2 0.6 constant_dynamic-update-slice_fusion.24
  26.4 0.6 constant_dynamic-update-slice_fusion.22
  27.0 0.6 constant_dynamic-update-slice_fusion.21
  27.6 0.6 constant_dynamic-update-slice_fusion.20
  28.3 0.6 constant_dynamic-update-slice_fusion.19
  28.9 0.6 constant_dynamic-update-slice_fusion.18
  29.5 0.6 constant_dynamic-update-slice_fusion.17
  30.1 0.6 constant_dynamic-update-slice_fusion.16
  30.8 0.6 constant_dynamic-update-slice_fusion.15
  31.4 0.6 constant_dynamic-update-slice_fusion.14
  32.0 0.6 constant_dynamic-update-slice_fusion.13
  32.6 0.6 constant_dynamic-update-slice_fusion.12
  33.3 0.6 constant_dynamic-update-slice_fusion.11
  33.9 0.6 constant_dynamic-update-slice_fusion.10
  34.5 0.6 constant_dynamic-update-slice_fusion.9
  35.8 0.6 constant_dynamic-update-slice_fusion.7
  36.4 0.6 constant_dynamic-update-slice_fusion.6
  37.0 0.6 constant_dynamic-update-slice_fusion.5
  37.6 0.6 constant_dynamic-update-slice_fusion.4
  38.3 0.6 constant_dynamic-update-slice_fusion.3
  38.9 0.6 constant_dynamic-update-slice_fusion.2
  39.5 0.6 constant_dynamic-update-slice_fusion.1
  40.1 0.6 constant_dynamic-update-slice_fusion
  40.8 11.7 %all-to-all-start.4 = ((bf16[32,1,224,128]{3,2,1,0:T(8,128)(2,1)}), bf16[32,1,224,128]{3,2,1,0:T(8,128)(2,1)S(1)}, u32[]{:S(2)}, u32[]{:S(2)}) async-start(bf16[32,1,224,128]{3,2,1,0:T(8,128)(2,1)} %constant_dynamic-update-slice_fusion), calls=%async_computation.4 | async-start | bytes 3670016 | tf_op jit(solution)/shard_map/all_to_all | solution.py:89
  52.9 43.4 %all-to-all-done.4 = bf16[32,1,224,128]{3,2,1,0:T(8,128)(2,1)S(1)} async-done(((bf16[32,1,224,128]{3,2,1,0:T(8,128)(2,1)}), bf16[32,1,224,128]{3,2,1,0:T(8,128)(2,1)S(1)}, u32[]{:S(2)}, u32[]{:S(2)}) %all-to-all-start.4) | async-done | bytes 1835040 | tf_op jit(solution)/shard_map/all_to_all | solution.py:89
  96.3 1.3 copy-done.4
  97.6 6.7 %all-to-all-start.2 = ((bf16[32,224,128]{2,1,0:T(8,128)(2,1)}), bf16[32,224,128]{2,1,0:T(8,128)(2,1)S(1)}, u32[]{:S(2)}, u32[]{:S(2)}) async-start(bf16[32,224,128]{2,1,0:T(8,128)(2,1)} %get-tuple-element.6), calls=%async_computation.2 | async-start | bytes 3670016 | tf_op jit(solution)/shard_map/all_to_all | solution.py:72
  105.7 13.4 %all-gather.1 = bf16[8,1,896]{2,1,0:T(2,128)(2,1)S(1)} all-gather(bf16[1,1,896]{2,1,0:T(2,128)(2,1)S(1)} %reshape.208), channel_id=2, replica_groups=mesh['expert'=32,'tensor'=8] {'tensor'}, dimensions={0}, use_global_device_ids=true | all-gather | bytes 16128 | tf_op jit(solution)/shard_map/all_gather | solution.py:107
  119.2 13.6 %all_gather.6 = bf16[32,7168]{1,0:T(8,128)(2,1)S(1)} all-gather(bf16[32,896]{1,0:T(8,128)(2,1)S(1)} %copy-done.7), channel_id=1, replica_groups=mesh['expert'=32,'tensor'=8] {'tensor'}, dimensions={1}, use_global_device_ids=true | all-gather | bytes 516096 | tf_op jit(solution)/shard_map/all_gather | solution.py:106
  133.2 20.7 %scatter_custom_fusion = bf16[576,7168]{1,0:T(8,128)(2,1)} fusion(s32[256]{0:T(256)S(1)} %bitcast.194, bf16[]{:T(256)} %constant.57.clone.1, bf16[32,7168]{1,0:T(8,128)(2,1)S(1)} %fusion.20, s32[1024]{0:T(1024)S(1)} %pad_clamp_fusion.2), kind=kCustom, calls=%fused_computation.8 | custom fusion | bytes 8257538 | tf_op jit(solution)/shard_map/scatter | solution.py:118
  153.9 10.4 %all_to_all.52 = bf16[32,18,7168]{2,1,0:T(8,128)(2,1)} reshape(bf16[576,7168]{1,0:T(8,128)(2,1)} %scatter_custom_fusion) | data formatting | bytes 16515072 | tf_op jit(solution)/shard_map/all_to_all | solution.py:120
  164.3 251.9 %all_to_all.68 = bf16[32,18,7168]{2,1,0:T(8,128)(2,1)} all-to-all(bf16[32,18,7168]{2,1,0:T(8,128)(2,1)} %all_to_all.52), channel_id=1, replica_groups=mesh['expert'=32,'tensor'=8] {'expert'}, dimensions={0} | all-to-all | bytes 16515072 | tf_op jit(solution)/shard_map/all_to_all | solution.py:120
  416.3 5.6 all-to-all-start.3
  422.1 10.5 %all_to_all.54 = bf16[576,7168]{1,0:T(8,128)(2,1)} reshape(bf16[32,18,7168]{2,1,0:T(8,128)(2,1)} %all_to_all.68) | data formatting | bytes 16515072 | tf_op jit(solution)/shard_map/all_to_all | solution.py:120
  432.6 6.1 %fusion.40 = f32[576,128]{1,0:T(8,128)S(1)} fusion(bf16[576,7168]{1,0:T(8,128)(2,1)} %all_to_all.54, bf16[7168,128]{1,0:T(8,128)(2,1)} %bitcast.186), kind=kOutput, calls=%fused_computation.144 | convolution fusion | flops 1056964608 | bytes 10387456 | tf_op jit(solution)/shard_map/dot_general | solution.py:121
  438.7 27.3 %all-to-all-done.3 = bf16[32,224,128]{2,1,0:T(8,128)(2,1)S(1)} async-done(((bf16[32,224,128]{2,1,0:T(8,128)(2,1)}), bf16[32,224,128]{2,1,0:T(8,128)(2,1)S(1)}, u32[]{:S(2)}, u32[]{:S(2)}) %all-to-all-start.3) | async-done | bytes 1835040 | tf_op jit(solution)/shard_map/all_to_all | solution.py:79
  466.0 13.6 %convolution_convert_fusion = bf16[576,7168]{1,0:T(8,128)(2,1)} fusion(bf16[7168,128]{1,0:T(8,128)(2,1)} %bitcast.188, bf16[576,7168]{1,0:T(8,128)(2,1)} %all_to_all.54, bf16[7168,128]{1,0:T(8,128)(2,1)S(1)} %bitcast.185, f32[576,128]{1,0:T(8,128)S(1)} %fusion.40), kind=kOutput, calls=%fused_computation.7 | convolution fusion | flops 2118500352 | bytes 20480000 | tf_op jit(solution)/shard_map/dot_general | solution.py:124
  479.7 12.4 %copy.44 = bf16[576,7168]{0,1:T(8,128)(2,1)} copy(bf16[576,7168]{1,0:T(8,128)(2,1)} %convolution_convert_fusion) | data formatting | bytes 16515072
  492.1 0.6 copy-done.12
  493.0 3.0 fusion.39
  496.0 3.0 fusion.13
  499.0 0.9 copy.37
  499.9 3.6 all-to-all-start
  503.5 46.4 %reduce-scatter.4.cloned.1.call-done = bf16[896,576]{1,0:T(8,128)(2,1)} async-done(((bf16[7168,576]{1,0:T(8,128)(2,1)}), bf16[896,576]{1,0:T(8,128)(2,1)}) %reduce-scatter.4.cloned.1.call-update) | async-done | bytes 1032208
  549.9 1.7 copy.45
  551.6 1.3 all_to_all.58
  552.9 10.2 %all-to-all-start.5 = ((bf16[32,18,896]{2,1,0:T(8,128)(2,1)}), bf16[32,18,896]{2,1,0:T(8,128)(2,1)S(1)}, u32[]{:S(2)}, u32[]{:S(2)}) async-start(bf16[32,18,896]{2,1,0:T(8,128)(2,1)} %all_to_all.58), calls=%async_computation.5 | async-start | bytes 2752512 | tf_op jit(solution)/shard_map/all_to_all | solution.py:130
  563.7 0.7 copy.55
  564.4 33.3 %all-to-all-done.5 = bf16[32,18,896]{2,1,0:T(8,128)(2,1)S(1)} async-done(((bf16[32,18,896]{2,1,0:T(8,128)(2,1)}), bf16[32,18,896]{2,1,0:T(8,128)(2,1)S(1)}, u32[]{:S(2)}, u32[]{:S(2)}) %all-to-all-start.5) | async-done | bytes 1032224 | tf_op jit(solution)/shard_map/all_to_all | solution.py:130
  598.0 1.2 gather_fusion
  599.2 1.0 fusion.21
  600.2 1.2 copy.90
  601.4 0.9 copy-done.1
  (65 shorter events, 6.8 us)
Async XLA Ops:
  7.2 2.1 copy-start
  10.3 3.7 copy-start.5
  40.8 11.8 %copy-start.9 = (s32[32,8]{0,1:T(8,128)S(1)}, s32[32,8]{0,1:T(8,128)}, u32[]{:S(2)}) copy-start(s32[32,8]{0,1:T(8,128)} %param.21) | copy-start | bytes 3076
  40.8 11.9 %copy-start.11 = (s32[32]{0:T(128)S(1)}, s32[32]{0:T(128)}, u32[]{:S(2)}) copy-start(s32[32]{0:T(128)} %param.23) | copy-start | bytes 388
  40.8 55.5 %all-to-all-start.4 = ((bf16[32,1,224,128]{3,2,1,0:T(8,128)(2,1)}), bf16[32,1,224,128]{3,2,1,0:T(8,128)(2,1)S(1)}, u32[]{:S(2)}, u32[]{:S(2)}) async-start(bf16[32,1,224,128]{3,2,1,0:T(8,128)(2,1)} %constant_dynamic-update-slice_fusion), calls=%async_computation.4 | async-start | bytes 3670016 | tf_op jit(solution)/shard_map/all_to_all | solution.py:89
  96.3 1.3 copy-start.4
  96.3 9.3 %copy-start.10 = (bf16[896]{0:T(1024)(128)(2,1)S(1)}, bf16[896]{0:T(1024)(128)(2,1)}, u32[]{:S(2)}) copy-start(bf16[896]{0:T(1024)(128)(2,1)} %param.20) | copy-start | bytes 5380
  96.3 22.9 %copy-start.7 = (bf16[32,896]{1,0:T(8,128)(2,1)S(1)}, bf16[32,896]{1,0:T(8,128)(2,1)}, u32[]{:S(2)}) copy-start(bf16[32,896]{1,0:T(8,128)(2,1)} %param.19) | copy-start | bytes 172036
  97.6 66.7 %all-to-all-start.2 = ((bf16[32,224,128]{2,1,0:T(8,128)(2,1)}), bf16[32,224,128]{2,1,0:T(8,128)(2,1)S(1)}, u32[]{:S(2)}, u32[]{:S(2)}) async-start(bf16[32,224,128]{2,1,0:T(8,128)(2,1)} %get-tuple-element.6), calls=%async_computation.2 | async-start | bytes 3670016 | tf_op jit(solution)/shard_map/all_to_all | solution.py:72
  164.3 251.9 %copy-start.2 = (bf16[32,224,128]{2,1,0:T(8,128)(2,1)}, bf16[32,224,128]{2,1,0:T(8,128)(2,1)S(1)}, u32[]{:S(2)}) copy-start(bf16[32,224,128]{2,1,0:T(8,128)(2,1)S(1)} %all-to-all-done.2) | copy-start | bytes 5505028
  416.3 49.8 %all-to-all-start.3 = ((bf16[32,224,128]{2,1,0:T(8,128)(2,1)}), bf16[32,224,128]{2,1,0:T(8,128)(2,1)S(1)}, u32[]{:S(2)}, u32[]{:S(2)}) async-start(bf16[32,224,128]{2,1,0:T(8,128)(2,1)} %get-tuple-element.7), calls=%async_computation.3 | async-start | bytes 3670016 | tf_op jit(solution)/shard_map/all_to_all | solution.py:79
  421.8 128.1 %reduce-scatter.4.cloned.1.call-start = ((), (), s32[]{:S(2)}) async-start(), calls=%async_computation.7 | async-start | bytes 10321920
  492.1 0.7 copy-start.12
  492.1 1.0 copy-start.13
  499.9 53.0 %all-to-all-start = ((bf16[4,64,512]{2,0,1:T(4,128)(2,1)}), bf16[4,64,512]{2,0,1:T(4,128)(2,1)S(1)}, u32[]{:S(2)}, u32[]{:S(2)}) async-start(bf16[4,64,512]{2,0,1:T(4,128)(2,1)} %copy.37), calls=%async_computation | async-start | bytes 524288 | tf_op jit(solution)/shard_map/all_to_all | solution.py:95
  552.9 10.3 %copy-start.8 = (s32[32,8]{0,1:T(8,128)S(1)}, s32[32,8]{0,1:T(8,128)}, u32[]{:S(2)}) copy-start(s32[32,8]{0,1:T(8,128)} %param.22) | copy-start | bytes 3076
  552.9 10.6 %copy-start.6 = (bf16[8,512,128]{2,1,0:T(8,128)(2,1)S(1)}, bf16[8,512,128]{2,1,0:T(8,128)(2,1)}, u32[]{:S(2)}) copy-start(bf16[8,512,128]{2,1,0:T(8,128)(2,1)} %param.18) | copy-start | bytes 3145732
  552.9 44.8 %all-to-all-start.5 = ((bf16[32,18,896]{2,1,0:T(8,128)(2,1)}), bf16[32,18,896]{2,1,0:T(8,128)(2,1)S(1)}, u32[]{:S(2)}, u32[]{:S(2)}) async-start(bf16[32,18,896]{2,1,0:T(8,128)(2,1)} %all_to_all.58), calls=%async_computation.5 | async-start | bytes 2752512 | tf_op jit(solution)/shard_map/all_to_all | solution.py:130
  598.0 2.2 copy-start.3
  600.2 2.1 copy-start.1
Sparse Core Ops, SparseCore 0:
  492.2 57.6 reduce-scatter.3
